TPU v7x, 32 devices: a whole 2x2x4 slice. The times are simulated.
32 devices in a mesh: dp: 8 (over y, x, core), tensor: 4 (over z).
Axes of the slice: x: 2, y: 2, z: 4, core: 2. Of those that a mesh axis runs over, the one named last changes fastest.
Arguments:
- block_input: float32 [12544, 512], P(('dp', 'tensor')), as said below
- cotangent: float32 [12544, 512], P(('dp', 'tensor')), may hold values from -6 to 6
- w_qkv: bfloat16 [2, 512, 3, 512], P(None, 'dp', None, 'tensor'), may hold values from -0.25 to 0.25
- b_qv: bfloat16 [2, 2, 512], P(None, None, 'tensor'), may hold values from -3 to 3
- bias_table: bfloat16 [2, 169, 16], P(None, None, 'tensor'), may hold values from -4 to 4
- w_proj: bfloat16 [2, 512, 512], P(None, 'tensor', 'dp'), may hold values from -0.75 to 0.75
- w_fc1: bfloat16 [2, 512, 2048], P(None, 'dp', 'tensor'), may hold values from -0.25 to 0.25
- b_fc1: bfloat16 [2, 2048], P(None, 'tensor'), may hold values from -3 to 3
- w_fc2: bfloat16 [2, 2048, 512], P(None, 'tensor', 'dp'), may hold values from -0.1875 to 0.1875
- norm_params: bfloat16 [2, 6, 512], P(None, None, 'dp'), as said below
- rel_index: int32 [49, 49], replicated, may hold values from 0 to 168, as said below
- shift_perm: int32 [196], replicated, may hold values from 0 to 195, as said below
- shift_mask: int32 [4, 49, 49], replicated, may hold values from 0 to 1, as said below
Outputs:
- block_output: float32 [12544, 512], P(('dp', 'tensor'))
- d_block_input: float32 [12544, 512], P(('dp', 'tensor'))
- d_w_qkv: float32 [2, 512, 3, 512], P(None, 'dp', None, 'tensor')
- d_b_qv: float32 [2, 2, 512], P(None, None, 'tensor')
- d_bias_table: float32 [2, 169, 16], P(None, None, 'tensor')
- d_w_proj: float32 [2, 512, 512], P(None, 'tensor', 'dp')
- d_w_fc1: float32 [2, 512, 2048], P(None, 'dp', 'tensor')
- d_b_fc1: float32 [2, 2048], P(None, 'tensor')
- d_w_fc2: float32 [2, 2048, 512], P(None, 'tensor', 'dp')
- d_norm_params: float32 [2, 6, 512], P(None, None, 'dp')
Inputs may be any that keep to these rules, and one draw needn't show every extreme that they name: `block_input`: standard normal scaled by a factor per token and a factor per feature. `norm_params`: rows 0 and 3 are positive gains. `rel_index`: two pairs of window positions have equal entries exactly when they have the same row offset and the same column offset; every value appears. A permutation: the image is rolled cyclically by amounts of 1 to 6 tokens, drawn once, along both grid dimensions, and cut into windows; window-ordered position j of the rolled image holds the token whose window-ordered position is shift_perm[j]. `shift_mask`: 1 where two positions of a window of the rolled image of shift_perm lie in different regions of the shifted-window partition for that roll, else 0; zero on the diagonal.
All inputs are finite; a program needn't handle non-finite values.
Results may differ from a plain program's by a relative error of at most 0.022.
Values may be sent and summed in bfloat16 or wider, within the bound.
No kernel may reach another device: no remote copies, remote signals or barrier semaphores. Data moves between devices by JAX's collectives and lax.ppermute only.
A program may use at most 192 MiB of HBM per device.

v0:
```python
import jax
import jax.numpy as jnp
from jax import lax
from jax.sharding import PartitionSpec as P

D = 512
HEAD_DIM = 32
WTOK = 49
ITOK = 196
NWIN = 4
RELS = 169
EPS = 1e-05
MASKED = -100.0
ROOT_HALF = 0.7071067811865476
ROOT_TWO_PI = 2.5066282746310002
full_precision = lax.Precision.HIGHEST


def gelu_value(inputs):
    return inputs * 0.5 * (1.0 + lax.erf(inputs * ROOT_HALF))


def gelu_slope(inputs):
    return (
        0.5 * (1.0 + lax.erf(inputs * ROOT_HALF))
        + inputs * jnp.exp(-0.5 * inputs * inputs) / ROOT_TWO_PI
    )


def layer_norm(hidden, norm_gain, offset):
    row_mean = jnp.mean(hidden, axis=-1, keepdims=True)
    centred = hidden - row_mean
    inv_std = lax.rsqrt(jnp.mean(centred * centred, axis=-1, keepdims=True) + EPS)
    normed = centred * inv_std
    return (normed * norm_gain + offset, normed, inv_std)


def norm_back(grad_rows, normed, inv_std, norm_gain):
    scaled = grad_rows * norm_gain
    centred_grad = (
        scaled
        - jnp.mean(scaled, axis=-1, keepdims=True)
        - normed * jnp.mean(scaled * normed, axis=-1, keepdims=True)
    )
    return inv_std * centred_grad


def inner_rows(left_side, right_side):
    return lax.dot_general(
        left_side, right_side, (((0,), (0,)), ((), ())), preferred_element_type=jnp.float32
    )


def times_transposed(left_side, right_side):
    return lax.dot_general(
        left_side, right_side, (((1,), (1,)), ((), ())), preferred_element_type=jnp.float32
    )


def rel_lookup(rel_index):
    flat_cells = rel_index.reshape(-1)
    return (flat_cells[:, None] == jnp.arange(RELS, dtype=jnp.int32)[None, :]).astype(jnp.float32)


def position_bias(lookup, pos_table):
    head_count = pos_table.shape[-1]
    flat_bias = jnp.dot(lookup, pos_table.astype(jnp.float32), precision=full_precision)
    return flat_bias.reshape(WTOK, WTOK, head_count).transpose(2, 0, 1)


def window_scores(query_blocks, key_blocks, pos_bias, mask_term):
    scores = jnp.einsum(
        "inqhe,inkhe->inhqk", query_blocks, key_blocks, preferred_element_type=jnp.float32
    )
    scores = scores + pos_bias[None, None]
    if mask_term is not None:
        scores = scores + mask_term[None, :, None]
    return scores


def spread_rows(values):
    return lax.all_gather(values, "tensor", axis=0, tiled=True)


def spread_grads(values):
    return lax.all_gather(values, "tensor", axis=0, tiled=True)


def branch_sum(values, weight):
    return lax.psum_scatter(
        jnp.dot(values, weight, preferred_element_type=jnp.float32).astype(jnp.bfloat16),
        "tensor",
        scatter_dimension=0,
        tiled=True,
    ).astype(jnp.float32)


def back_sum(values, weight):
    return lax.psum_scatter(
        times_transposed(values, weight).astype(jnp.bfloat16),
        "tensor",
        scatter_dimension=0,
        tiled=True,
    ).astype(jnp.float32)


def forward_layer(hidden, weights, lookup, mask_term, reorder):
    w_qkv, b_qv, pos_table, w_proj, w_fc1, b_fc1, w_fc2, norm_rows = weights
    norm_rows = norm_rows.astype(jnp.float32)
    local_width = w_qkv.shape[-1]
    head_count = local_width // HEAD_DIM
    score_scale = HEAD_DIM ** (-0.5)
    ln_first, normed_first, inv_first = layer_norm(hidden, norm_rows[0], norm_rows[1])
    gathered = spread_rows(ln_first.astype(jnp.bfloat16))
    image_count = gathered.shape[0] // ITOK
    arranged = gathered.reshape(image_count, ITOK, D)
    if reorder is not None:
        arranged = jnp.take(arranged, reorder[0], axis=1)
    permuted_rows = arranged.reshape(image_count * ITOK, D)
    projected = jnp.dot(
        permuted_rows, w_qkv.reshape(D, 3 * local_width), preferred_element_type=jnp.float32
    )
    projected = projected.reshape(-1, 3, local_width)
    biases = b_qv.astype(jnp.float32)
    query_rows = ((projected[:, 0] + biases[0]) * score_scale).astype(jnp.bfloat16)
    key_rows = projected[:, 1].astype(jnp.bfloat16)
    value_rows = (projected[:, 2] + biases[1]).astype(jnp.bfloat16)
    block_shape = (image_count, NWIN, WTOK, head_count, HEAD_DIM)
    query_blocks = query_rows.reshape(block_shape)
    key_blocks = key_rows.reshape(block_shape)
    value_blocks = value_rows.reshape(block_shape)
    pos_bias = position_bias(lookup, pos_table)
    scores = window_scores(query_blocks, key_blocks, pos_bias, mask_term)
    row_peak = jnp.max(scores, axis=-1, keepdims=True)
    log_total = row_peak + jnp.log(jnp.sum(jnp.exp(scores - row_peak), axis=-1, keepdims=True))
    soft_weights = jnp.exp(scores - log_total).astype(jnp.bfloat16)
    mixed = jnp.einsum(
        "inhqk,inkhe->inqhe", soft_weights, value_blocks, preferred_element_type=jnp.float32
    ).astype(jnp.bfloat16)
    mixed = mixed.reshape(image_count, ITOK, local_width)
    if reorder is not None:
        mixed = jnp.take(mixed, reorder[1], axis=1)
    mixed = mixed.reshape(image_count * ITOK, local_width)
    residual = hidden + branch_sum(mixed, w_proj) + norm_rows[2]
    ln_second, normed_second, inv_second = layer_norm(residual, norm_rows[3], norm_rows[4])
    spread = spread_rows(ln_second.astype(jnp.bfloat16))
    pre_active = jnp.dot(spread, w_fc1, preferred_element_type=jnp.float32) + b_fc1.astype(
        jnp.float32
    )
    active = gelu_value(pre_active).astype(jnp.bfloat16)
    result = residual + branch_sum(active, w_fc2) + norm_rows[5]
    kept_state = (
        normed_first,
        inv_first,
        permuted_rows,
        query_blocks,
        key_blocks,
        value_blocks,
        log_total,
        mixed,
        normed_second,
        inv_second,
        spread,
        pre_active,
        active,
    )
    return (result, kept_state)


def backward_layer(out_grad, kept_state, weights, lookup, mask_term, reorder):
    (
        normed_first,
        inv_first,
        permuted_rows,
        query_blocks,
        key_blocks,
        value_blocks,
        log_total,
        mixed,
        normed_second,
        inv_second,
        spread,
        pre_active,
        active,
    ) = kept_state
    w_qkv, b_qv, pos_table, w_proj, w_fc1, b_fc1, w_fc2, norm_rows = weights
    norm_rows = norm_rows.astype(jnp.float32)
    local_width = w_qkv.shape[-1]
    head_count = local_width // HEAD_DIM
    score_scale = HEAD_DIM ** (-0.5)
    image_count = permuted_rows.shape[0] // ITOK
    grad_rounded = spread_grads(out_grad.astype(jnp.bfloat16))
    d_fc2 = inner_rows(active, grad_rounded)
    d_active = times_transposed(grad_rounded, w_fc2)
    d_pre = d_active * gelu_slope(pre_active)
    d_bias_fc1 = jnp.sum(d_pre, axis=0)
    d_pre_rounded = d_pre.astype(jnp.bfloat16)
    d_fc1 = inner_rows(spread, d_pre_rounded)
    d_spread = back_sum(d_pre_rounded, w_fc1)
    d_residual = out_grad + norm_back(d_spread, normed_second, inv_second, norm_rows[3])
    mix_grad = spread_grads(d_residual.astype(jnp.bfloat16))
    d_proj = inner_rows(mixed, mix_grad)
    d_mixed = (
        times_transposed(mix_grad, w_proj)
        .astype(jnp.bfloat16)
        .reshape(image_count, ITOK, local_width)
    )
    if reorder is not None:
        d_mixed = jnp.take(d_mixed, reorder[0], axis=1)
    d_mixed_blocks = d_mixed.reshape(image_count, NWIN, WTOK, head_count, HEAD_DIM)
    pos_bias = position_bias(lookup, pos_table)
    scores = window_scores(query_blocks, key_blocks, pos_bias, mask_term)
    soft_exact = jnp.exp(scores - log_total)
    d_values = jnp.einsum(
        "inhqk,inqhe->inkhe",
        soft_exact.astype(jnp.bfloat16),
        d_mixed_blocks,
        preferred_element_type=jnp.float32,
    )
    d_soft = jnp.einsum(
        "inqhe,inkhe->inhqk", d_mixed_blocks, value_blocks, preferred_element_type=jnp.float32
    )
    d_scores = soft_exact * (d_soft - jnp.sum(soft_exact * d_soft, axis=-1, keepdims=True))
    score_total = jnp.sum(d_scores, axis=(0, 1)).reshape(head_count, WTOK * WTOK)
    d_table = jnp.dot(lookup.T, score_total.T, precision=full_precision)
    d_scores_rounded = d_scores.astype(jnp.bfloat16)
    d_query = (
        jnp.einsum(
            "inhqk,inkhe->inqhe", d_scores_rounded, key_blocks, preferred_element_type=jnp.float32
        )
        * score_scale
    )
    d_keys = jnp.einsum(
        "inhqk,inqhe->inkhe", d_scores_rounded, query_blocks, preferred_element_type=jnp.float32
    )
    d_query = d_query.reshape(-1, local_width)
    d_keys = d_keys.reshape(-1, local_width)
    d_values = d_values.reshape(-1, local_width)
    d_bias_qv = jnp.stack([jnp.sum(d_query, axis=0), jnp.sum(d_values, axis=0)])
    d_joint = (
        jnp.stack([d_query, d_keys, d_values], axis=1)
        .astype(jnp.bfloat16)
        .reshape(-1, 3 * local_width)
    )
    d_qkv = inner_rows(permuted_rows, d_joint).reshape(D, 3, local_width)
    if reorder is not None:
        d_joint = jnp.take(
            d_joint.reshape(image_count, ITOK, 3 * local_width), reorder[1], axis=1
        ).reshape(image_count * ITOK, 3 * local_width)
    d_normed = back_sum(d_joint, w_qkv.reshape(D, 3 * local_width))
    d_hidden = d_residual + norm_back(d_normed, normed_first, inv_first, norm_rows[0])
    norm_grads = jnp.stack(
        [
            jnp.sum(d_normed * normed_first, axis=0),
            jnp.sum(d_normed, axis=0),
            jnp.sum(d_residual, axis=0),
            jnp.sum(d_spread * normed_second, axis=0),
            jnp.sum(d_spread, axis=0),
            jnp.sum(out_grad, axis=0),
        ]
    )
    return (d_hidden, (d_qkv, d_proj, d_fc1, d_fc2), (d_bias_qv, d_table, d_bias_fc1), norm_grads)


def join_two(first_item, second_item):
    return jnp.concatenate([first_item, second_item], axis=0)


def body(
    block_input,
    cotangent,
    w_qkv,
    b_qv,
    bias_table,
    w_proj,
    w_fc1,
    b_fc1,
    w_fc2,
    norm_params,
    rel_index,
    shift_perm,
    shift_mask,
):
    full_qkv, full_proj, full_fc1, full_fc2, norm_rows = (
        lax.all_gather(w_qkv, "dp", axis=1, tiled=True),
        lax.all_gather(w_proj, "dp", axis=2, tiled=True),
        lax.all_gather(w_fc1, "dp", axis=1, tiled=True),
        lax.all_gather(w_fc2, "dp", axis=2, tiled=True),
        lax.all_gather(norm_params, "dp", axis=2, tiled=True),
    )
    head_bias, pos_table, fc1_bias = (b_qv, bias_table, b_fc1)
    inverse = jnp.zeros((ITOK,), jnp.int32).at[shift_perm].set(jnp.arange(ITOK, dtype=jnp.int32))
    reorder = (shift_perm, inverse)
    lookup = rel_lookup(rel_index)
    mask_term = shift_mask.astype(jnp.float32) * MASKED

    def weights_of(layer_index):
        return (
            full_qkv[layer_index],
            head_bias[layer_index],
            pos_table[layer_index],
            full_proj[layer_index],
            full_fc1[layer_index],
            fc1_bias[layer_index],
            full_fc2[layer_index],
            norm_rows[layer_index],
        )

    first_out, kept_first = forward_layer(block_input, weights_of(0), lookup, None, None)
    second_out, kept_second = forward_layer(first_out, weights_of(1), lookup, mask_term, reorder)
    kept_layers = (kept_first, kept_second)
    layer_masks = (None, mask_term)
    layer_orders = (None, reorder)
    grad_now = cotangent
    finished = []
    for layer_index in (1, 0):
        grad_now, weight_grads, small_grads, norm_grads = backward_layer(
            grad_now,
            kept_layers[layer_index],
            weights_of(layer_index),
            lookup,
            layer_masks[layer_index],
            layer_orders[layer_index],
        )
        d_qkv, d_proj, d_fc1, d_fc2 = weight_grads
        d_bias_qv, d_table, d_bias_fc1 = small_grads
        norm_sum = lax.psum(norm_grads, "tensor")
        shards = (d_qkv[None], d_proj[None], d_fc1[None], d_fc2[None], norm_sum[None])
        finished.append((shards, (d_bias_qv[None], d_table[None], d_bias_fc1[None])))
    later_layer = finished[0]
    earlier_layer = finished[1]
    joined_qkv, joined_proj, joined_fc1, joined_fc2, joined_norms = jax.tree.map(
        join_two, earlier_layer[0], later_layer[0]
    )
    small_qv, small_table, small_fc1 = jax.tree.map(join_two, earlier_layer[1], later_layer[1])
    joined_qkv, joined_proj, joined_fc1, joined_fc2, joined_norms = (
        lax.psum_scatter(
            joined_qkv.astype(jnp.bfloat16), "dp", scatter_dimension=1, tiled=True
        ).astype(jnp.float32),
        lax.psum_scatter(
            joined_proj.astype(jnp.bfloat16), "dp", scatter_dimension=2, tiled=True
        ).astype(jnp.float32),
        lax.psum_scatter(
            joined_fc1.astype(jnp.bfloat16), "dp", scatter_dimension=1, tiled=True
        ).astype(jnp.float32),
        lax.psum_scatter(
            joined_fc2.astype(jnp.bfloat16), "dp", scatter_dimension=2, tiled=True
        ).astype(jnp.float32),
        lax.psum_scatter(
            joined_norms.astype(jnp.bfloat16), "dp", scatter_dimension=2, tiled=True
        ).astype(jnp.float32),
    )
    d_bias_qv, d_table, d_bias_fc1 = lax.psum((small_qv, small_table, small_fc1), "dp")
    return (
        second_out,
        grad_now,
        joined_qkv,
        d_bias_qv,
        d_table,
        joined_proj,
        joined_fc1,
        d_bias_fc1,
        joined_fc2,
        joined_norms,
    )


def solution(mesh):
    in_specs = (
        P(("dp", "tensor"), None),
        P(("dp", "tensor"), None),
        P(None, "dp", None, "tensor"),
        P(None, None, "tensor"),
        P(None, None, "tensor"),
        P(None, "tensor", "dp"),
        P(None, "dp", "tensor"),
        P(None, "tensor"),
        P(None, "tensor", "dp"),
        P(None, None, "dp"),
        P(),
        P(),
        P(),
    )
    out_specs = (
        P(("dp", "tensor"), None),
        P(("dp", "tensor"), None),
        P(None, "dp", None, "tensor"),
        P(None, None, "tensor"),
        P(None, None, "tensor"),
        P(None, "tensor", "dp"),
        P(None, "dp", "tensor"),
        P(None, "tensor"),
        P(None, "tensor", "dp"),
        P(None, None, "dp"),
    )
    return jax.shard_map(body, mesh=mesh, in_specs=in_specs, out_specs=out_specs, check_vma=False)
```

profile of v0, /device:TPU:0, one launch (start us, length us, event | category | flops | bytes accessed | tf_op | source)
XLA Modules:
  0.0 1039.6 jit_solution(14769519194201761679)
XLA Ops:
  22.8 11.3 %slice_reduce_fusion.6 = (f32[512]{0:T(512)S(1)}, f32[512]{0:T(512)S(1)}, f32[512]{0:T(512)S(1)}, f32[512]{0:T(512)S(1)}, f32[512]{0:T(512)S(1)}, /*index=5*/f32[512]{0:T(512)S(1)}) fusion(f32[1,6,512]{1,0,2:T(1,128)S(1)} %get-tuple-element.115), kind=kLoop, calls=%fused_computation.203 | loop fusion | bytes 24576 | tf_op jit(solution)/shard_map/slice | solution.py:151
  58.8 14.3 %all-gather.11.cloned.1.call-done = bf16[1568,512]{1,0:T(8,128)(2,1)} async-done(((bf16[392,512]{1,0:T(8,128)(2,1)}), bf16[1568,512]{1,0:T(8,128)(2,1)}) %all-gather.11.cloned.1.call-update) | async-done | bytes 1605648 | tf_op jit(solution)/shard_map/all_gather | solution.py:82
  108.5 34.3 %reduce-scatter.14.cloned.1.call-done = bf16[392,512]{1,0:T(8,128)(2,1)} async-done(((bf16[1568,512]{1,0:T(8,128)(2,1)}), bf16[392,512]{1,0:T(8,128)(2,1)}) %reduce-scatter.14.cloned.1.call-update) | async-done | bytes 401424 | tf_op jit(solution)/shard_map/reduce_scatter | solution.py:90
  146.5 35.2 %all-gather.13.cloned.1.call-done = bf16[1568,512]{1,0:T(8,128)(2,1)} async-done(((bf16[392,512]{1,0:T(8,128)(2,1)}), bf16[1568,512]{1,0:T(8,128)(2,1)}) %all-gather.13.cloned.1.call-update) | async-done | bytes 1605648 | tf_op jit(solution)/shard_map/all_gather | solution.py:82
  186.2 19.4 %all-gather.17.cloned.1.call-done = bf16[2,512,512]{1,2,0:T(8,128)(2,1)} async-done(((bf16[2,512,64]{1,2,0:T(8,128)(2,1)}), bf16[2,512,512]{1,2,0:T(8,128)(2,1)}) %all-gather.17.cloned.1.call-update) | async-done | bytes 1048592 | tf_op jit(solution)/shard_map/all_gather | solution.py:288
  209.3 11.7 %slice_reduce_fusion = (f32[512]{0:T(512)}, f32[512]{0:T(512)}, f32[512]{0:T(512)}, f32[512]{0:T(512)}, f32[512]{0:T(512)S(1)}, /*index=5*/f32[512]{0:T(512)S(1)}) fusion(f32[1,6,512]{1,0,2:T(1,128)S(1)} %get-tuple-element.116), kind=kLoop, calls=%fused_computation.196 | loop fusion | bytes 24576 | tf_op jit(solution)/shard_map/slice | solution.py:151
  221.1 23.9 %reduce-scatter.16.cloned.1.call-done = bf16[392,512]{1,0:T(8,128)(2,1)} async-done(((bf16[1568,512]{1,0:T(8,128)(2,1)}), bf16[392,512]{1,0:T(8,128)(2,1)}) %reduce-scatter.16.cloned.1.call-update) | async-done | bytes 401424 | tf_op jit(solution)/shard_map/reduce_scatter | solution.py:90
  254.3 29.5 %all-gather.19.cloned.1.call-done = bf16[1568,512]{1,0:T(8,128)(2,1)} async-done(((bf16[392,512]{1,0:T(8,128)(2,1)}), bf16[1568,512]{1,0:T(8,128)(2,1)}) %all-gather.19.cloned.1.call-update) | async-done | bytes 1605648 | tf_op jit(solution)/shard_map/all_gather | solution.py:82
  343.9 34.9 %reduce-scatter.18.cloned.1.call-done = bf16[392,512]{1,0:T(8,128)(2,1)} async-done(((bf16[1568,512]{1,0:T(8,128)(2,1)}), bf16[392,512]{1,0:T(8,128)(2,1)}) %reduce-scatter.18.cloned.1.call-update) | async-done | bytes 401424 | tf_op jit(solution)/shard_map/reduce_scatter | solution.py:90
  385.4 35.5 %all-gather.21.cloned.1.call-done = bf16[1568,512]{1,0:T(8,128)(2,1)} async-done(((bf16[392,512]{1,0:T(8,128)(2,1)}), bf16[1568,512]{1,0:T(8,128)(2,1)}) %all-gather.21.cloned.1.call-update) | async-done | bytes 1605648 | tf_op jit(solution)/shard_map/all_gather | solution.py:82
  426.1 33.3 %all-gather.23.cloned.1.call-done = bf16[1568,512]{1,0:T(8,128)(2,1)} async-done(((bf16[392,512]{1,0:T(8,128)(2,1)}), bf16[1568,512]{1,0:T(8,128)(2,1)}) %all-gather.23.cloned.1.call-update) | async-done | bytes 1605648 | tf_op jit(solution)/shard_map/all_gather | solution.py:86
  471.9 31.0 %reduce-scatter.22.cloned.1.call-done = bf16[392,512]{1,0:T(8,128)(2,1)} async-done(((bf16[1568,512]{1,0:T(8,128)(2,1)}), bf16[392,512]{1,0:T(8,128)(2,1)}) %reduce-scatter.22.cloned.1.call-update) | async-done | bytes 401424 | tf_op jit(solution)/shard_map/reduce_scatter | solution.py:99
  506.1 33.7 %reduce-scatter.20.cloned.1.call-done = bf16[392,512]{1,0:T(8,128)(2,1)} async-done(((bf16[1568,512]{1,0:T(8,128)(2,1)}), bf16[392,512]{1,0:T(8,128)(2,1)}) %reduce-scatter.20.cloned.1.call-update) | async-done | bytes 401424 | tf_op jit(solution)/shard_map/reduce_scatter | solution.py:90
  544.9 36.5 %all-gather.25.cloned.1.call-done = bf16[1568,512]{1,0:T(8,128)(2,1)} async-done(((bf16[392,512]{1,0:T(8,128)(2,1)}), bf16[1568,512]{1,0:T(8,128)(2,1)}) %all-gather.25.cloned.1.call-update) | async-done | bytes 1605648 | tf_op jit(solution)/shard_map/all_gather | solution.py:86
  641.7 34.9 %reduce-scatter.24.cloned.1.call-done = bf16[392,512]{1,0:T(8,128)(2,1)} async-done(((bf16[1568,512]{1,0:T(8,128)(2,1)}), bf16[392,512]{1,0:T(8,128)(2,1)}) %reduce-scatter.24.cloned.1.call-update) | async-done | bytes 401424 | tf_op jit(solution)/shard_map/reduce_scatter | solution.py:99
  682.4 36.3 %all-gather.27.cloned.1.call-done = bf16[1568,512]{1,0:T(8,128)(2,1)} async-done(((bf16[392,512]{1,0:T(8,128)(2,1)}), bf16[1568,512]{1,0:T(8,128)(2,1)}) %all-gather.27.cloned.1.call-update) | async-done | bytes 1605648 | tf_op jit(solution)/shard_map/all_gather | solution.py:86
  727.4 34.9 %reduce-scatter.26.cloned.1.call-done = bf16[392,512]{1,0:T(8,128)(2,1)} async-done(((bf16[1568,512]{1,0:T(8,128)(2,1)}), bf16[392,512]{1,0:T(8,128)(2,1)}) %reduce-scatter.26.cloned.1.call-update) | async-done | bytes 401424 | tf_op jit(solution)/shard_map/reduce_scatter | solution.py:99
  784.4 20.1 %all-gather.29.cloned.1.call-done = bf16[1568,512]{1,0:T(8,128)(2,1)} async-done(((bf16[392,512]{1,0:T(8,128)(2,1)}), bf16[1568,512]{1,0:T(8,128)(2,1)}) %all-gather.29.cloned.1.call-update) | async-done | bytes 1605648 | tf_op jit(solution)/shard_map/all_gather | solution.py:86
  855.5 23.5 %all-reduce.2 = (f32[2,2,128]{2,1,0:T(2,128)}, f32[2,169,4]{1,2,0:T(4,128)}, f32[2,512]{1,0:T(2,128)}) all-reduce(f32[2,2,128]{2,1,0:T(2,128)S(1)} %pad_maximum_fusion.7, f32[2,169,4]{1,2,0:T(4,128)S(1)} %pad_maximum_fusion.5, f32[2,512]{1,0:T(2,128)S(1)} %pad_maximum_fusion.6), channel_id=1, replica_groups=mesh['dp'=8,'tensor'=4] {'dp'}, use_global_device_ids=true, to_apply=%region_36.38 | all-reduce | flops 2888 | bytes 23104 | tf_op jit(solution)/shard_map/psum | solution.py:353
  879.1 24.2 %all-reduce.7.cloned.1.call-done = (bf16[2,128,512]{1,0,2:T(2,128)(2,1)}, bf16[2,512,512]{1,0,2:T(2,128)(2,1)}) async-done(((bf16[2,128,512]{1,0,2:T(2,128)(2,1)}, bf16[2,512,512]{1,0,2:T(2,128)(2,1)}), (bf16[2,128,512]{1,0,2:T(2,128)(2,1)}, bf16[2,512,512]{1,0,2:T(2,128)(2,1)})) %all-reduce.7.cloned.1.call-update) | async-done | bytes 1310736
  906.4 34.0 %reduce-scatter.30.cloned.1.call-done = bf16[2,64,3,128]{3,1,2,0:T(8,128)(2,1)} async-done(((bf16[2,512,3,128]{3,1,2,0:T(8,128)(2,1)}), bf16[2,64,3,128]{3,1,2,0:T(8,128)(2,1)}) %reduce-scatter.30.cloned.1.call-update) | async-done | bytes 98320 | tf_op jit(solution)/shard_map/reduce_scatter | solution.py:337
  942.0 36.5 %reduce-scatter.28.cloned.1.call-done = bf16[392,512]{1,0:T(8,128)(2,1)} async-done(((bf16[1568,512]{1,0:T(8,128)(2,1)}), bf16[392,512]{1,0:T(8,128)(2,1)}) %reduce-scatter.28.cloned.1.call-update) | async-done | bytes 401424 | tf_op jit(solution)/shard_map/reduce_scatter | solution.py:99
  980.2 17.0 %all-reduce.3 = (bf16[6,512]{1,0:T(8,128)(2,1)S(1)}, bf16[6,512]{1,0:T(8,128)(2,1)S(1)}) all-reduce(f32[6,512]{1,0:T(8,128)S(1)} %stack.87, f32[6,512]{1,0:T(8,128)S(1)} %stack.80), channel_id=1, replica_groups=mesh['dp'=8,'tensor'=4] {'tensor'}, use_global_device_ids=true, to_apply=%region_59.61 | all-reduce | flops 6144 | bytes 36864 | tf_op jit(solution)/shard_map/psum | solution.py:327
  999.5 30.8 %reduce-scatter.34.cloned.1.call-done = bf16[64,12]{1,0:T(8,128)(2,1)} async-done(((bf16[512,12]{1,0:T(8,128)(2,1)}), bf16[64,12]{1,0:T(8,128)(2,1)}) %reduce-scatter.34.cloned.1.call-update) | async-done | bytes 1552
  (473 shorter events, 344.5 us)
Async XLA Ops:
  8.0 65.1 %all-gather.11.cloned.1.call-start = ((), (), s32[]{:S(2)}) async-start(), calls=%async_computation.11 | async-start | bytes 2007040 | tf_op jit(solution)/shard_map/all_gather | solution.py:82
  35.1 107.8 %reduce-scatter.14.cloned.1.call-start = ((), (), s32[]{:S(2)}) async-start(), calls=%async_computation.12 | async-start | bytes 2007040 | tf_op jit(solution)/shard_map/reduce_scatter | solution.py:90
  107.9 38.6 %all-gather.15.cloned.1.call-start = ((), (), s32[]{:S(2)}) async-start(), calls=%async_computation.14 | async-start | bytes 1179648 | tf_op jit(solution)/shard_map/all_gather | solution.py:287
  108.4 73.2 %all-gather.13.cloned.1.call-start = ((), (), s32[]{:S(2)}) async-start(), calls=%async_computation.13 | async-start | bytes 2007040 | tf_op jit(solution)/shard_map/all_gather | solution.py:82
  145.3 60.3 %all-gather.17.cloned.1.call-start = ((), (), s32[]{:S(2)}) async-start(), calls=%async_computation.15 | async-start | bytes 1179648 | tf_op jit(solution)/shard_map/all_gather | solution.py:288
  145.9 99.1 %reduce-scatter.16.cloned.1.call-start = ((), (), s32[]{:S(2)}) async-start(), calls=%async_computation.16 | async-start | bytes 2007040 | tf_op jit(solution)/shard_map/reduce_scatter | solution.py:90
  208.9 75.0 %all-gather.19.cloned.1.call-start = ((), (), s32[]{:S(2)}) async-start(), calls=%async_computation.17 | async-start | bytes 2007040 | tf_op jit(solution)/shard_map/all_gather | solution.py:82
  247.5 131.3 %reduce-scatter.18.cloned.1.call-start = ((), (), s32[]{:S(2)}) async-start(), calls=%async_computation.18 | async-start | bytes 2007040 | tf_op jit(solution)/shard_map/reduce_scatter | solution.py:90
  343.9 77.0 %all-gather.21.cloned.1.call-start = ((), (), s32[]{:S(2)}) async-start(), calls=%async_computation.19 | async-start | bytes 2007040 | tf_op jit(solution)/shard_map/all_gather | solution.py:82
  384.4 75.0 %all-gather.23.cloned.1.call-start = ((), (), s32[]{:S(2)}) async-start(), calls=%async_computation.21 | async-start | bytes 2007040 | tf_op jit(solution)/shard_map/all_gather | solution.py:86
  384.9 117.9 %reduce-scatter.22.cloned.1.call-start = ((), (), s32[]{:S(2)}) async-start(), calls=%async_computation.22 | async-start | bytes 2007040 | tf_op jit(solution)/shard_map/reduce_scatter | solution.py:99
  468.0 71.9 %reduce-scatter.20.cloned.1.call-start = ((), (), s32[]{:S(2)}) async-start(), calls=%async_computation.20 | async-start | bytes 2007040 | tf_op jit(solution)/shard_map/reduce_scatter | solution.py:90
  471.8 109.5 %all-gather.25.cloned.1.call-start = ((), (), s32[]{:S(2)}) async-start(), calls=%async_computation.23 | async-start | bytes 2007040 | tf_op jit(solution)/shard_map/all_gather | solution.py:86
  544.8 131.8 %reduce-scatter.24.cloned.1.call-start = ((), (), s32[]{:S(2)}) async-start(), calls=%async_computation.24 | async-start | bytes 2007040 | tf_op jit(solution)/shard_map/reduce_scatter | solution.py:99
  641.7 77.1 %all-gather.27.cloned.1.call-start = ((), (), s32[]{:S(2)}) async-start(), calls=%async_computation.25 | async-start | bytes 2007040 | tf_op jit(solution)/shard_map/all_gather | solution.py:86
  682.3 80.0 %reduce-scatter.26.cloned.1.call-start = ((), (), s32[]{:S(2)}) async-start(), calls=%async_computation.26 | async-start | bytes 2007040 | tf_op jit(solution)/shard_map/reduce_scatter | solution.py:99
  727.4 77.1 %all-gather.29.cloned.1.call-start = ((), (), s32[]{:S(2)}) async-start(), calls=%async_computation.27 | async-start | bytes 2007040 | tf_op jit(solution)/shard_map/all_gather | solution.py:86
  768.1 84.5 %reduce-scatter.32.cloned.1.call-start = ((), (), s32[]{:S(2)}) async-start(), calls=%async_computation.30 | async-start | bytes 1179648 | tf_op jit(solution)/shard_map/reduce_scatter | solution.py:343
  784.4 118.9 %all-reduce.7.cloned.1.call-start = ((), (), s32[]{:S(2)}) async-start(), calls=%async_computation.32 | async-start | bytes 2621440
  842.0 98.4 %reduce-scatter.30.cloned.1.call-start = ((), (), s32[]{:S(2)}) async-start(), calls=%async_computation.29 | async-start | bytes 884736 | tf_op jit(solution)/shard_map/reduce_scatter | solution.py:337
  845.8 132.8 %reduce-scatter.28.cloned.1.call-start = ((), (), s32[]{:S(2)}) async-start(), calls=%async_computation.28 | async-start | bytes 2007040 | tf_op jit(solution)/shard_map/reduce_scatter | solution.py:99
  849.6 129.0 %copy-start.64 = (f32[512]{0:T(512)S(1)}, f32[512]{0:T(512)}, u32[]{:S(2)}) copy-start(f32[512]{0:T(512)} %copy-done.63) | copy-start | bytes 6148
  849.6 180.7 %reduce-scatter.34.cloned.1.call-start = ((), (), s32[]{:S(2)}) async-start(), calls=%async_computation.31 | async-start | bytes 147456
  854.6 143.6 %copy-start.20 = (f32[392,512]{1,0:T(8,128)S(1)}, f32[392,512]{1,0:T(8,128)}, u32[]{:S(2)}) copy-start(f32[392,512]{1,0:T(8,128)} %copy-done.19) | copy-start | bytes 2408452
  (106 other events, 1835.3 us)
Sparse Core Ops, SparseCore 0:
  35.2 37.8 all-gather.10
  108.0 34.7 reduce-scatter.13
  209.0 35.9 reduce-scatter.15
  384.5 36.3 all-gather.20
  422.9 36.4 all-gather.22
  544.9 36.3 all-gather.24
  641.8 34.7 reduce-scatter.23
  727.5 34.8 reduce-scatter.25
Sparse Core Ops, SparseCore 1:
  110.3 22.1 all-gather.14
  145.4 36.2 all-gather.12
  183.5 22.1 all-gather.16
  247.6 36.2 all-gather.18
  344.0 34.8 reduce-scatter.17
  468.0 34.8 reduce-scatter.21
  505.0 34.7 reduce-scatter.19
  682.4 36.3 all-gather.26
  768.2 36.3 all-gather.28
  807.7 34.8 reduce-scatter.31
  845.6 57.6 all-reduce.6
  906.4 34.0 reduce-scatter.29
  942.6 35.9 reduce-scatter.27
  998.3 31.9 reduce-scatter.33
where the time goes:
time: 1050 us; the launch traced here: 1040 us
  waiting for transfers between devices  615 us (59%)
  local copies, waits for them, and re-layouts  177 us (17%)
  matrix products  95.6 us (9%)
  blocking collectives  70.2 us (7%)
  other arithmetic  61.5 us (6%)
  between operations  18.3 us (2%)
    reduce_scatter x4, waiting for transfers between devices, back_sum(): lax.psum_scatter(times_transposed(values, weight).astype(jnp.bfloat16), '...  137 us
    reduce_scatter x4, waiting for transfers between devices, branch_sum(): lax.psum_scatter(jnp.dot(values, weight, preferred_element_type=jnp.float...  127 us
    all_gather x4, waiting for transfers between devices, spread_grads(): return lax.all_gather(values, 'tensor', axis=0, tiled=True)  126 us
    all_gather x4, waiting for transfers between devices, spread_rows(): return lax.all_gather(values, 'tensor', axis=0, tiled=True)  114 us
    unnamed x24, waiting for transfers between devices  56.9 us
    reduce_scatter x1, waiting for transfers between devices, body(): lax.psum_scatter(joined_qkv.astype(jnp.bfloat16), 'dp', scatter_dimension...  34 us
    dot_general x8, matrix products, times_transposed(): lax.dot_general(left_side, right_side, (((1,), (1,)), ((), ())), preferre...  25.2 us
    psum x1, blocking collectives, body(): lax.psum((small_qv, small_table, small_fc1), 'dp')  23.5 us
  transfers between devices with their start and end apart: 22, of which 20 were waited for; matrix products, arithmetic and copies ran while one was open for 11% of the time, Pallas kernels for 0%

commit v1 on v0

--- a/solution.py
+++ b/solution.py
@@ -1,3 +1,4 @@
+import functools
 import jax
 import jax.numpy as jnp
 from jax import lax
@@ -16,6 +17,35 @@
 full_precision = lax.Precision.HIGHEST
 
 
+def _refer_domain(page, comm_axis):
+    tall, new, y2 = (jax.lax.axis_size(comm_axis), jax.lax.axis_index(comm_axis), page.shape[0])
+    parts_seen = tuple((dd * tall if i0 == 0 else dd for i0, dd in enumerate(page.shape)))
+    local_next = lax.dynamic_update_slice_in_dim(
+        jnp.zeros(parts_seen, page.dtype), page, new * y2, axis=0
+    )
+    heard = state_next = page
+    k0 = 1
+    while k0 < tall // 2 + 1:
+        heard = jax.lax.ppermute(
+            heard, comm_axis, tuple(((i0, (i0 + 1) % tall) for i0 in range(tall)))
+        )
+        local_next = lax.dynamic_update_slice_in_dim(
+            local_next, heard, (new - k0) % tall * y2, axis=0
+        )
+        if 2 * k0 < tall:
+            state_next = jax.lax.ppermute(
+                state_next, comm_axis, tuple(((i0, (i0 - 1) % tall) for i0 in range(tall)))
+            )
+            local_next = lax.dynamic_update_slice_in_dim(
+                local_next, state_next, (new + k0) % tall * y2, axis=0
+            )
+        k0 += 1
+    return local_next
+
+
+number_sector = functools.partial(_refer_domain, comm_axis="tensor")
+
+
 def gelu_value(inputs):
     return inputs * 0.5 * (1.0 + lax.erf(inputs * ROOT_HALF))
 
@@ -83,7 +113,7 @@
 
 
 def spread_grads(values):
-    return lax.all_gather(values, "tensor", axis=0, tiled=True)
+    return number_sector(values)
 
 
 def branch_sum(values, weight):

time: 1050 us -> 1000 us (0.952)
  waiting for transfers between devices: 615 us -> 538 us
  starting transfers between devices: 1.75 us -> 38.1 us
  matrix products: 95.6 us -> 84.9 us
    all_gather x4 -> x0, waiting for transfers between devices: 126 us -> none  [spread_grads(): return lax.all_gather(values, 'tensor', axis=0, tiled=True)]
    ppermute x0 -> x12, waiting for transfers between devices: none -> 87.6 us  [the longest x8 78.7 us: _refer_domain(): jax.lax.ppermute(heard, comm_axis, tuple(((i0, (i0 + 1) % tall) for i0 in...]
    ppermute x0 -> x12, starting transfers between devices: none -> 36.5 us  [the longest x8 22.8 us: _refer_domain(): jax.lax.ppermute(heard, comm_axis, tuple(((i0, (i0 + 1) % tall) for i0 in...]
    all_gather x4, waiting for transfers between devices: 114 us -> 79.8 us  [spread_rows(): return lax.all_gather(values, 'tensor', axis=0, tiled=True)]
    reduce_scatter x4, waiting for transfers between devices: 127 us -> 139 us  [branch_sum(): lax.psum_scatter(jnp.dot(values, weight, preferred_element_type=jnp.float...]
    unnamed x24 -> x20, waiting for transfers between devices: 56.9 us -> 50.9 us
    slice x2 -> x1, local copies, waits for them, and re-layouts: 23 us -> 21.2 us  [forward_layer(): result = residual + branch_sum(active, w_fc2) + norm_rows[5]]
  transfers between devices with their start and end apart: 22 -> 30, of which waited for: 20 -> 27; matrix products, arithmetic and copies ran while one was open for 11% -> 11% of each run, Pallas kernels for 0% -> 0%
where the time goes in v1:
time: 1000 us; the launch traced here: 995 us
  waiting for transfers between devices  538 us (54%)
  local copies, waits for them, and re-layouts  186 us (19%)
  matrix products  84.9 us (8%)
  blocking collectives  70.2 us (7%)
  other arithmetic  58.9 us (6%)
  starting transfers between devices  38.1 us (4%)
  between operations  18.1 us (2%)
    reduce_scatter x4, waiting for transfers between devices, branch_sum(): lax.psum_scatter(jnp.dot(values, weight, preferred_element_type=jnp.float...  139 us
    reduce_scatter x4, waiting for transfers between devices, back_sum(): lax.psum_scatter(times_transposed(values, weight).astype(jnp.bfloat16), '...  127 us
    all_gather x4, waiting for transfers between devices, spread_rows(): return lax.all_gather(values, 'tensor', axis=0, tiled=True)  79.8 us
    ppermute x8, waiting for transfers between devices, _refer_domain(): jax.lax.ppermute(heard, comm_axis, tuple(((i0, (i0 + 1) % tall) for i0 in...  78.7 us
    unnamed x20, waiting for transfers between devices  50.9 us
    reduce_scatter x1, waiting for transfers between devices, body(): lax.psum_scatter(joined_qkv.astype(jnp.bfloat16), 'dp', scatter_dimension...  34 us
    psum x1, blocking collectives, body(): lax.psum((small_qv, small_table, small_fc1), 'dp')  23.5 us
    ppermute x8, starting transfers between devices, _refer_domain(): jax.lax.ppermute(heard, comm_axis, tuple(((i0, (i0 + 1) % tall) for i0 in...  22.8 us
  transfers between devices with their start and end apart: 30, of which 27 were waited for; matrix products, arithmetic and copies ran while one was open for 11% of the time, Pallas kernels for 0%

profile of v1, /device:TPU:0, one launch (start us, length us, event | category | flops | bytes accessed | tf_op | source)
XLA Modules:
  0.0 994.7 jit_solution(4152438101857558174)
XLA Ops:
  8.9 10.8 %all_gather.27 = bf16[2,6,512]{1,0,2:T(2,128)(2,1)S(1)} all-gather(bf16[2,6,64]{1,0,2:T(2,128)(2,1)S(1)} %copy.165), channel_id=1, replica_groups=mesh['dp'=8,'tensor'=4] {'dp'}, dimensions={2}, use_global_device_ids=true | all-gather | bytes 13824 | tf_op jit(solution)/shard_map/all_gather | solution.py:319
  20.5 21.2 %slice_reduce_fusion = (f32[512]{0:T(512)}, f32[512]{0:T(512)}, f32[512]{0:T(512)}, f32[512]{0:T(512)}, f32[512]{0:T(512)}, /*index=5*/f32[512]{0:T(512)}, f32[5...) fusion(f32[1,6,512]{1,0,2:T(1,128)S(1)} %get-tuple-element.123, ...), kind=kLoop, calls=%fused_computation.196 | loop fusion | bytes 49152 | tf_op jit(solution)/shard_map/slice | solution.py:181
  42.9 10.5 %all_gather.29 = bf16[2,512,3,128]{3,0,2,1:T(2,128)(2,1)S(1)} all-gather(bf16[2,64,3,128]{3,0,2,1:T(2,128)(2,1)S(1)} %copy.166), channel_id=1, replica_groups=mesh['dp'=8,'tensor'=4] {'dp'}, dimensions={1}, use_global_device_ids=true | all-gather | bytes 884736 | tf_op jit(solution)/shard_map/all_gather | solution.py:315
  66.4 14.3 %all-gather.7.cloned.1.call-done = bf16[1568,512]{1,0:T(8,128)(2,1)} async-done(((bf16[392,512]{1,0:T(8,128)(2,1)}), bf16[1568,512]{1,0:T(8,128)(2,1)}) %all-gather.7.cloned.1.call-update) | async-done | bytes 1605648 | tf_op jit(solution)/shard_map/all_gather | solution.py:112
  114.5 34.3 %reduce-scatter.14.cloned.1.call-done = bf16[392,512]{1,0:T(8,128)(2,1)} async-done(((bf16[1568,512]{1,0:T(8,128)(2,1)}), bf16[392,512]{1,0:T(8,128)(2,1)}) %reduce-scatter.14.cloned.1.call-update) | async-done | bytes 401424 | tf_op jit(solution)/shard_map/reduce_scatter | solution.py:120
  153.4 34.8 %all-gather.9.cloned.1.call-done = bf16[1568,512]{1,0:T(8,128)(2,1)} async-done(((bf16[392,512]{1,0:T(8,128)(2,1)}), bf16[1568,512]{1,0:T(8,128)(2,1)}) %all-gather.9.cloned.1.call-update) | async-done | bytes 1605648 | tf_op jit(solution)/shard_map/all_gather | solution.py:112
  192.7 19.4 %all-gather.13.cloned.1.call-done = bf16[2,512,512]{1,2,0:T(8,128)(2,1)} async-done(((bf16[2,512,64]{1,2,0:T(8,128)(2,1)}), bf16[2,512,512]{1,2,0:T(8,128)(2,1)}) %all-gather.13.cloned.1.call-update) | async-done | bytes 1048592 | tf_op jit(solution)/shard_map/all_gather | solution.py:318
  215.5 36.1 %reduce-scatter.16.cloned.1.call-done = bf16[392,512]{1,0:T(8,128)(2,1)} async-done(((bf16[1568,512]{1,0:T(8,128)(2,1)}), bf16[392,512]{1,0:T(8,128)(2,1)}) %reduce-scatter.16.cloned.1.call-update) | async-done | bytes 401424 | tf_op jit(solution)/shard_map/reduce_scatter | solution.py:120
  260.6 29.8 %all-gather.15.cloned.1.call-done = bf16[1568,512]{1,0:T(8,128)(2,1)} async-done(((bf16[392,512]{1,0:T(8,128)(2,1)}), bf16[1568,512]{1,0:T(8,128)(2,1)}) %all-gather.15.cloned.1.call-update) | async-done | bytes 1605648 | tf_op jit(solution)/shard_map/all_gather | solution.py:112
  350.6 34.9 %reduce-scatter.18.cloned.1.call-done = bf16[392,512]{1,0:T(8,128)(2,1)} async-done(((bf16[1568,512]{1,0:T(8,128)(2,1)}), bf16[392,512]{1,0:T(8,128)(2,1)}) %reduce-scatter.18.cloned.1.call-update) | async-done | bytes 401424 | tf_op jit(solution)/shard_map/reduce_scatter | solution.py:120
  395.5 15.9 %collective-permute-done = bf16[392,512]{1,0:T(8,128)(2,1)} collective-permute-done((bf16[392,512]{1,0:T(8,128)(2,1)}, bf16[392,512]{1,0:T(8,128)(2,1)}, u32[]{:S(2)}, u32[]{:S(2)}) %collective-permute-start) | collective-permute-done | bytes 401440 | tf_op jit(solution)/shard_map/ppermute | solution.py:29
  411.4 10.4 %collective-permute-start.2 = (bf16[392,512]{1,0:T(8,128)(2,1)}, bf16[392,512]{1,0:T(8,128)(2,1)}, u32[]{:S(2)}, u32[]{:S(2)}) collective-permute-start(bf16[392,512]{1,0:T(8,128)(2,1)} %collective-permute-done), channel_id=1, source_target_pairs={{0,1},{1,2},{2,3},{3,0},{4,5},{5,6},{6,7},{7,4},{8,9},{9,10},{10,1... | collective-permute-start | bytes 1204232 | tf_op jit(solution)/shard_map/ppermute | solution.py:29
  431.7 12.5 %collective-permute-done.2 = bf16[392,512]{1,0:T(8,128)(2,1)} collective-permute-done((bf16[392,512]{1,0:T(8,128)(2,1)}, bf16[392,512]{1,0:T(8,128)(2,1)}, u32[]{:S(2)}, u32[]{:S(2)}) %collective-permute-start.2) | collective-permute-done | bytes 401440 | tf_op jit(solution)/shard_map/ppermute | solution.py:29
  462.7 31.7 %reduce-scatter.22.cloned.1.call-done = bf16[392,512]{1,0:T(8,128)(2,1)} async-done(((bf16[1568,512]{1,0:T(8,128)(2,1)}), bf16[392,512]{1,0:T(8,128)(2,1)}) %reduce-scatter.22.cloned.1.call-update) | async-done | bytes 401424 | tf_op jit(solution)/shard_map/reduce_scatter | solution.py:129
  497.7 33.8 %reduce-scatter.20.cloned.1.call-done = bf16[392,512]{1,0:T(8,128)(2,1)} async-done(((bf16[1568,512]{1,0:T(8,128)(2,1)}), bf16[392,512]{1,0:T(8,128)(2,1)}) %reduce-scatter.20.cloned.1.call-update) | async-done | bytes 401424 | tf_op jit(solution)/shard_map/reduce_scatter | solution.py:120
  554.4 10.2 %collective-permute-done.5 = bf16[392,512]{1,0:T(8,128)(2,1)S(1)} collective-permute-done((bf16[392,512]{1,0:T(8,128)(2,1)S(1)}, bf16[392,512]{1,0:T(8,128)(2,1)S(1)}, u32[]{:S(2)}, u32[]{:S(2)}) %collective-permute-start.5) | collective-permute-done | bytes 401440 | tf_op jit(solution)/shard_map/ppermute | solution.py:29
  623.1 34.1 %reduce-scatter.24.cloned.1.call-done = bf16[392,512]{1,0:T(8,128)(2,1)} async-done(((bf16[1568,512]{1,0:T(8,128)(2,1)}), bf16[392,512]{1,0:T(8,128)(2,1)}) %reduce-scatter.24.cloned.1.call-update) | async-done | bytes 401424 | tf_op jit(solution)/shard_map/reduce_scatter | solution.py:129
  706.0 24.8 %reduce-scatter.26.cloned.1.call-done = bf16[392,512]{1,0:T(8,128)(2,1)} async-done(((bf16[1568,512]{1,0:T(8,128)(2,1)}), bf16[392,512]{1,0:T(8,128)(2,1)}) %reduce-scatter.26.cloned.1.call-update) | async-done | bytes 401424 | tf_op jit(solution)/shard_map/reduce_scatter | solution.py:129
  816.3 23.5 %all-reduce.2 = (f32[2,2,128]{2,1,0:T(2,128)}, f32[2,169,4]{1,2,0:T(4,128)}, f32[2,512]{1,0:T(2,128)}) all-reduce(f32[2,2,128]{2,1,0:T(2,128)S(1)} %pad_maximum_fusion.7, f32[2,169,4]{1,2,0:T(4,128)S(1)} %pad_maximum_fusion.5, f32[2,512]{1,0:T(2,128)S(1)} %pad_maximum_fusion.6), channel_id=1, replica_groups=mesh['dp'=8,'tensor'=4] {'dp'}, use_global_device_ids=true, to_apply=%region_36.38 | all-reduce | flops 2888 | bytes 23104 | tf_op jit(solution)/shard_map/psum | solution.py:383
  839.8 18.8 %all-reduce.7.cloned.1.call-done = (bf16[2,128,512]{1,0,2:T(2,128)(2,1)}, bf16[2,512,512]{1,0,2:T(2,128)(2,1)}) async-done(((bf16[2,128,512]{1,0,2:T(2,128)(2,1)}, bf16[2,512,512]{1,0,2:T(2,128)(2,1)}), (bf16[2,128,512]{1,0,2:T(2,128)(2,1)}, bf16[2,512,512]{1,0,2:T(2,128)(2,1)})) %all-reduce.7.cloned.1.call-update) | async-done | bytes 1310736
  861.7 34.0 %reduce-scatter.30.cloned.1.call-done = bf16[2,64,3,128]{3,1,2,0:T(8,128)(2,1)} async-done(((bf16[2,512,3,128]{3,1,2,0:T(8,128)(2,1)}), bf16[2,64,3,128]{3,1,2,0:T(8,128)(2,1)}) %reduce-scatter.30.cloned.1.call-update) | async-done | bytes 98320 | tf_op jit(solution)/shard_map/reduce_scatter | solution.py:367
  897.3 36.6 %reduce-scatter.28.cloned.1.call-done = bf16[392,512]{1,0:T(8,128)(2,1)} async-done(((bf16[1568,512]{1,0:T(8,128)(2,1)}), bf16[392,512]{1,0:T(8,128)(2,1)}) %reduce-scatter.28.cloned.1.call-update) | async-done | bytes 401424 | tf_op jit(solution)/shard_map/reduce_scatter | solution.py:129
  935.5 17.0 %all-reduce.3 = (bf16[6,512]{1,0:T(8,128)(2,1)S(1)}, bf16[6,512]{1,0:T(8,128)(2,1)S(1)}) all-reduce(f32[6,512]{1,0:T(8,128)S(1)} %stack.87, f32[6,512]{1,0:T(8,128)S(1)} %stack.80), channel_id=1, replica_groups=mesh['dp'=8,'tensor'=4] {'tensor'}, use_global_device_ids=true, to_apply=%region_59.61 | all-reduce | flops 6144 | bytes 36864 | tf_op jit(solution)/shard_map/psum | solution.py:357
  954.8 30.8 %reduce-scatter.34.cloned.1.call-done = bf16[64,12]{1,0:T(8,128)(2,1)} async-done(((bf16[512,12]{1,0:T(8,128)(2,1)}), bf16[64,12]{1,0:T(8,128)(2,1)}) %reduce-scatter.34.cloned.1.call-update) | async-done | bytes 1552
  (517 shorter events, 396.4 us)
Async XLA Ops:
  8.0 72.7 %all-gather.7.cloned.1.call-start = ((), (), s32[]{:S(2)}) async-start(), calls=%async_computation.11 | async-start | bytes 2007040 | tf_op jit(solution)/shard_map/all_gather | solution.py:112
  42.7 106.1 %reduce-scatter.14.cloned.1.call-start = ((), (), s32[]{:S(2)}) async-start(), calls=%async_computation.12 | async-start | bytes 2007040 | tf_op jit(solution)/shard_map/reduce_scatter | solution.py:120
  113.8 39.6 %all-gather.11.cloned.1.call-start = ((), (), s32[]{:S(2)}) async-start(), calls=%async_computation.14 | async-start | bytes 1179648 | tf_op jit(solution)/shard_map/all_gather | solution.py:317
  114.4 73.7 %all-gather.9.cloned.1.call-start = ((), (), s32[]{:S(2)}) async-start(), calls=%async_computation.13 | async-start | bytes 2007040 | tf_op jit(solution)/shard_map/all_gather | solution.py:112
  151.8 60.3 %all-gather.13.cloned.1.call-start = ((), (), s32[]{:S(2)}) async-start(), calls=%async_computation.15 | async-start | bytes 1179648 | tf_op jit(solution)/shard_map/all_gather | solution.py:318
  152.4 99.2 %reduce-scatter.16.cloned.1.call-start = ((), (), s32[]{:S(2)}) async-start(), calls=%async_computation.16 | async-start | bytes 2007040 | tf_op jit(solution)/shard_map/reduce_scatter | solution.py:120
  215.4 75.0 %all-gather.15.cloned.1.call-start = ((), (), s32[]{:S(2)}) async-start(), calls=%async_computation.17 | async-start | bytes 2007040 | tf_op jit(solution)/shard_map/all_gather | solution.py:112
  254.0 131.4 %reduce-scatter.18.cloned.1.call-start = ((), (), s32[]{:S(2)}) async-start(), calls=%async_computation.18 | async-start | bytes 2007040 | tf_op jit(solution)/shard_map/reduce_scatter | solution.py:120
  350.5 96.5 %all-gather.17.cloned.1.call-start = ((), (), s32[]{:S(2)}) async-start(), calls=%async_computation.19 | async-start | bytes 2007040 | tf_op jit(solution)/shard_map/all_gather | solution.py:112
  389.2 105.2 %reduce-scatter.22.cloned.1.call-start = ((), (), s32[]{:S(2)}) async-start(), calls=%async_computation.21 | async-start | bytes 2007040 | tf_op jit(solution)/shard_map/reduce_scatter | solution.py:129
  391.6 19.8 %collective-permute-start = (bf16[392,512]{1,0:T(8,128)(2,1)}, bf16[392,512]{1,0:T(8,128)(2,1)}, u32[]{:S(2)}, u32[]{:S(2)}) collective-permute-start(bf16[392,512]{1,0:T(8,128)(2,1)} %get-tuple-element.107), channel_id=1, source_target_pairs={{0,1},{1,2},{2,3},{3,0},{4,5},{5,6},{6,7},{7,4},{8,9},{9,10},{10,1... | collective-permute-start | bytes 1204232 | tf_op jit(solution)/shard_map/ppermute | solution.py:29
  391.7 38.2 %collective-permute-start.1 = (bf16[392,512]{1,0:T(8,128)(2,1)}, bf16[392,512]{1,0:T(8,128)(2,1)}, u32[]{:S(2)}, u32[]{:S(2)}) collective-permute-start(bf16[392,512]{1,0:T(8,128)(2,1)} %get-tuple-element.107), channel_id=1, source_target_pairs={{0,3},{1,0},{2,1},{3,2},{4,7},{5,4},{6,5},{7,6},{8,11},{9,8},{10,9... | collective-permute-start | bytes 1204232 | tf_op jit(solution)/shard_map/ppermute | solution.py:36
  411.4 32.8 %collective-permute-start.2 = (bf16[392,512]{1,0:T(8,128)(2,1)}, bf16[392,512]{1,0:T(8,128)(2,1)}, u32[]{:S(2)}, u32[]{:S(2)}) collective-permute-start(bf16[392,512]{1,0:T(8,128)(2,1)} %collective-permute-done), channel_id=1, source_target_pairs={{0,1},{1,2},{2,3},{3,0},{4,5},{5,6},{6,7},{7,4},{8,9},{9,10},{10,1... | collective-permute-start | bytes 1204232 | tf_op jit(solution)/shard_map/ppermute | solution.py:29
  458.9 72.6 %reduce-scatter.20.cloned.1.call-start = ((), (), s32[]{:S(2)}) async-start(), calls=%async_computation.20 | async-start | bytes 2007040 | tf_op jit(solution)/shard_map/reduce_scatter | solution.py:120
  462.7 194.6 %reduce-scatter.24.cloned.1.call-start = ((), (), s32[]{:S(2)}) async-start(), calls=%async_computation.22 | async-start | bytes 2007040 | tf_op jit(solution)/shard_map/reduce_scatter | solution.py:129
  535.2 19.2 %collective-permute-start.4 = (bf16[392,512]{1,0:T(8,128)(2,1)S(1)}, bf16[392,512]{1,0:T(8,128)(2,1)S(1)}, u32[]{:S(2)}, u32[]{:S(2)}) collective-permute-start(bf16[392,512]{1,0:T(8,128)(2,1)S(1)} %get-tuple-element.105), channel_id=1, source_target_pairs={{0,3},{1,0},{2,1},{3,2},{4,7},{5,4},{6,5},{7,6},{8,11},{9,8},{10,9... | collective-permute-start | bytes 1204232 | tf_op jit(solution)/shard_map/ppermute | solution.py:36
  623.1 107.7 %reduce-scatter.26.cloned.1.call-start = ((), (), s32[]{:S(2)}) async-start(), calls=%async_computation.23 | async-start | bytes 2007040 | tf_op jit(solution)/shard_map/reduce_scatter | solution.py:129
  661.2 19.2 %collective-permute-start.7 = (bf16[392,512]{1,0:T(8,128)(2,1)S(1)}, bf16[392,512]{1,0:T(8,128)(2,1)S(1)}, u32[]{:S(2)}, u32[]{:S(2)}) collective-permute-start(bf16[392,512]{1,0:T(8,128)(2,1)S(1)} %get-tuple-element.103), channel_id=1, source_target_pairs={{0,3},{1,0},{2,1},{3,2},{4,7},{5,4},{6,5},{7,6},{8,11},{9,8},{10,9... | collective-permute-start | bytes 1204232 | tf_op jit(solution)/shard_map/ppermute | solution.py:36
  696.6 116.6 %reduce-scatter.32.cloned.1.call-start = ((), (), s32[]{:S(2)}) async-start(), calls=%async_computation.26 | async-start | bytes 1179648 | tf_op jit(solution)/shard_map/reduce_scatter | solution.py:373
  737.1 24.2 %collective-permute-start.10 = (bf16[392,512]{1,0:T(8,128)(2,1)}, bf16[392,512]{1,0:T(8,128)(2,1)}, u32[]{:S(2)}, u32[]{:S(2)}) collective-permute-start(bf16[392,512]{1,0:T(8,128)(2,1)} %get-tuple-element.101), channel_id=1, source_target_pairs={{0,3},{1,0},{2,1},{3,2},{4,7},{5,4},{6,5},{7,6},{8,11},{9,8},{10,9... | collective-permute-start | bytes 1204232 | tf_op jit(solution)/shard_map/ppermute | solution.py:36
  759.8 98.7 %all-reduce.7.cloned.1.call-start = ((), (), s32[]{:S(2)}) async-start(), calls=%async_computation.28 | async-start | bytes 2621440
  802.5 93.3 %reduce-scatter.30.cloned.1.call-start = ((), (), s32[]{:S(2)}) async-start(), calls=%async_computation.25 | async-start | bytes 884736 | tf_op jit(solution)/shard_map/reduce_scatter | solution.py:367
  806.6 127.3 %reduce-scatter.28.cloned.1.call-start = ((), (), s32[]{:S(2)}) async-start(), calls=%async_computation.24 | async-start | bytes 2007040 | tf_op jit(solution)/shard_map/reduce_scatter | solution.py:129
  810.3 175.2 %reduce-scatter.34.cloned.1.call-start = ((), (), s32[]{:S(2)}) async-start(), calls=%async_computation.27 | async-start | bytes 147456
  (123 other events, 1828.8 us)
Sparse Core Ops, SparseCore 0:
  42.8 37.8 all-gather.6
  114.0 34.7 reduce-scatter.13
  215.5 35.9 reduce-scatter.15
  389.3 57.6 all-gather.16
  459.0 35.4 reduce-scatter.21
  496.6 34.8 reduce-scatter.19
Sparse Core Ops, SparseCore 1:
  116.2 22.1 all-gather.10
  151.9 36.2 all-gather.8
  189.9 22.1 all-gather.12
  254.1 36.2 all-gather.14
  350.6 34.8 reduce-scatter.17
  623.2 34.1 reduce-scatter.23
  696.7 34.1 reduce-scatter.25
  759.9 36.4 reduce-scatter.31
  802.6 55.9 all-reduce.6
  861.7 34.0 reduce-scatter.29
  897.9 35.9 reduce-scatter.27
  953.6 31.9 reduce-scatter.33
